TPU v7x, 512 devices: a whole 4x4x16 slice. The times are simulated.
512 devices in a mesh: expert: 128 (over y, x_lo, z), half: 4 (over x_hi, core).
Axes of the slice: x: 4 (x_hi: 2, x_lo: 2; x = x_hi * 2 + x_lo), y: 4, z: 16, core: 2. Of those that a mesh axis runs over, the one named last changes fastest.
Arguments:
- tokens: bfloat16 [25088, 1024], P('expert', 'half'), may hold values from -128 to 128
- slot_params: bfloat16 [1024, 256], P('half'), may hold values from -0.5 to 0.5
- w_up: bfloat16 [128, 1024, 4096], P('expert', None, 'half'), may hold values from -0.1875 to 0.1875
- w_down: bfloat16 [128, 4096, 1024], P('expert', 'half'), may hold values from -0.09375 to 0.09375
- cotangent: bfloat16 [25088, 1024], P('expert', 'half'), may hold values from -6 to 6
Outputs:
- mixed: bfloat16 [25088, 1024], P('expert', 'half')
- grad_tokens: bfloat16 [25088, 1024], P('expert', 'half')
- grad_params: float32 [1024, 256], P('half')
All inputs are finite; a program needn't handle non-finite values.
Results may differ from a plain program's by a relative error of at most 0.017.
Values may be sent and summed in bfloat16 or wider, within the bound.
A program may use at most 64 MiB of HBM per device.

v0:
```python
import jax
import jax.numpy as jnp
from jax import lax
from jax.sharding import PartitionSpec as P

SEQ = 196
SLOTS = 2
EXPERT = ("y", "x_lo", "z")
HALF = ("x_hi", "core")


def gelu_grad(preact, upstream):
    pullback = jax.vjp(jax.nn.gelu, preact)[1]
    return pullback(upstream)[0]


def softmax_back(probabilities, upstream, over_axis):
    inner = jnp.sum(probabilities * upstream, axis=over_axis, keepdims=True)
    return probabilities * (upstream - inner)


def local(tokens, slot_params, w_up, w_down, cotangent):
    feat_quarter = tokens.shape[1]
    images = tokens.shape[0] // SEQ
    columns = slot_params.shape[1]
    experts = columns // SLOTS
    up_matrix = w_up[0]
    down_matrix = w_down[0]
    inputs = tokens.reshape(images, SEQ, feat_quarter)
    upstream = cotangent.reshape(images, SEQ, feat_quarter)
    partial_logits = jnp.einsum(
        "imf,fc->imc", inputs, slot_params, preferred_element_type=jnp.float32
    )
    logits = lax.psum(partial_logits, HALF)
    dispatch = jax.nn.softmax(logits, axis=1)
    combine = jax.nn.softmax(logits, axis=2)
    dispatch_bf = dispatch.astype(jnp.bfloat16).reshape(images, SEQ, experts, SLOTS)
    combine_bf = combine.astype(jnp.bfloat16).reshape(images, SEQ, experts, SLOTS)
    slot_in = jnp.einsum(
        "imes,imf->sife", dispatch_bf, inputs, preferred_element_type=jnp.float32
    ).astype(jnp.bfloat16)
    received = lax.all_to_all(slot_in, EXPERT, split_axis=3, concat_axis=3, tiled=True)
    up_slice = up_matrix
    preact = jnp.einsum(
        "sifr,fk->sirk",
        lax.all_gather(received, HALF, axis=2, tiled=True),
        up_slice,
        preferred_element_type=jnp.float32,
    )
    hidden = jax.nn.gelu(preact).astype(jnp.bfloat16)
    down_slice = down_matrix
    summed = lax.psum(
        jnp.einsum("kf,sirk->fsir", down_slice, hidden, preferred_element_type=jnp.float32).astype(
            jnp.bfloat16
        ),
        HALF,
    ).astype(jnp.float32)
    slot_out = lax.dynamic_slice_in_dim(
        summed, lax.axis_index(HALF) * feat_quarter, feat_quarter, 0
    )
    returned = lax.all_to_all(
        slot_out.astype(jnp.bfloat16), EXPERT, split_axis=3, concat_axis=3, tiled=True
    )
    mixed = jnp.einsum(
        "imes,fsie->imf", combine_bf, returned, preferred_element_type=jnp.float32
    ).astype(jnp.bfloat16)
    grad_slot_out = jnp.einsum(
        "imes,imf->sife", combine_bf, upstream, preferred_element_type=jnp.float32
    ).astype(jnp.bfloat16)
    combine_part = jnp.einsum(
        "imf,fsie->imes", upstream, returned, preferred_element_type=jnp.float32
    ).reshape(images, SEQ, columns)
    grad_combine = lax.psum(combine_part.astype(jnp.bfloat16), HALF).astype(jnp.float32)
    grad_received = lax.all_to_all(grad_slot_out, EXPERT, split_axis=3, concat_axis=3, tiled=True)
    down_slice = down_matrix
    grad_hidden = jnp.einsum(
        "sifr,kf->sirk",
        lax.all_gather(grad_received, HALF, axis=2, tiled=True),
        down_slice,
        preferred_element_type=jnp.float32,
    )
    grad_preact = gelu_grad(preact, grad_hidden).astype(jnp.bfloat16)
    up_slice = up_matrix
    summed_grad = lax.psum(
        jnp.einsum(
            "fk,sirk->fsir", up_slice, grad_preact, preferred_element_type=jnp.float32
        ).astype(jnp.bfloat16),
        HALF,
    ).astype(jnp.float32)
    grad_slot_in = lax.dynamic_slice_in_dim(
        summed_grad, lax.axis_index(HALF) * feat_quarter, feat_quarter, 0
    )
    grad_returned = lax.all_to_all(
        grad_slot_in.astype(jnp.bfloat16), EXPERT, split_axis=3, concat_axis=3, tiled=True
    )
    dispatch_part = jnp.einsum(
        "imf,fsie->imes", inputs, grad_returned, preferred_element_type=jnp.float32
    ).reshape(images, SEQ, columns)
    grad_dispatch = lax.psum(dispatch_part.astype(jnp.bfloat16), HALF).astype(jnp.float32)
    grad_logits = softmax_back(combine, grad_combine, 2) + softmax_back(dispatch, grad_dispatch, 1)
    grad_logit_bf = grad_logits.astype(jnp.bfloat16)
    token_term = jnp.einsum(
        "imes,fsie->imf", dispatch_bf, grad_returned, preferred_element_type=jnp.float32
    )
    logit_term = jnp.einsum(
        "imc,fc->imf", grad_logit_bf, slot_params, preferred_element_type=jnp.float32
    )
    grad_tokens = (token_term + logit_term).astype(jnp.bfloat16).reshape(images * SEQ, feat_quarter)
    params_part = jnp.einsum(
        "imf,imc->fc", inputs, grad_logit_bf, preferred_element_type=jnp.float32
    )
    grad_params = lax.psum(lax.psum(lax.psum(params_part, "z"), "y"), "x_lo")
    return (mixed.reshape(images * SEQ, feat_quarter), grad_tokens, grad_params)


def solution(mesh):
    mesh = jax.sharding.Mesh(mesh.devices.reshape(4, 2, 16, 2, 2), EXPERT + HALF)
    in_specs = (
        P(EXPERT, HALF),
        P(HALF, None),
        P(EXPERT, None, HALF),
        P(EXPERT, HALF, None),
        P(EXPERT, HALF),
    )
    out_specs = (P(EXPERT, HALF), P(EXPERT, HALF), P(HALF, None))
    return jax.shard_map(local, mesh=mesh, in_specs=in_specs, out_specs=out_specs, check_vma=False)
```

profile of v0, /device:TPU:1, one launch (start us, length us, event | category | flops | bytes accessed | tf_op | source)
XLA Modules:
  0.0 566.3 jit_solution(11431547479652277655)
XLA Ops:
  7.2 2.0 convolution_bitcast_fusion.3
  9.2 64.2 %all-reduce.9.cloned.1.call-done = f32[1,196,256]{2,1,0:T(8,128)} async-done(((f32[1,196,256]{2,1,0:T(8,128)}), f32[1,196,256]{2,1,0:T(8,128)}) %all-reduce.9.cloned.1.call-update) | async-done | bytes 200720 | tf_op jit(solution)/shard_map/psum | solution.py:34
  73.4 1.0 fusion.82
  74.5 1.1 fusion.60
  75.6 1.1 fusion.80
  78.1 16.6 %all-to-all-start = ((bf16[2,1,256,128]{2,0,1,3:T(2,128)(2,1)}), bf16[2,1,256,128]{2,0,1,3:T(2,128)(2,1)S(1)}, u32[]{:S(2)}, u32[]{:S(2)}) async-start(bf16[2,1,256,128]{2,0,1,3:T(2,128)(2,1)} %copy.37), calls=%async_computation | async-start | bytes 262144 | tf_op jit(solution)/shard_map/all_to_all | solution.py:42
  96.1 15.3 %all-to-all-done = bf16[2,1,256,128]{2,0,1,3:T(2,128)(2,1)S(1)} async-done(((bf16[2,1,256,128]{2,0,1,3:T(2,128)(2,1)}), bf16[2,1,256,128]{2,0,1,3:T(2,128)(2,1)S(1)}, u32[]{:S(2)}, u32[]{:S(2)}) %all-to-all-start) | async-done | bytes 131104 | tf_op jit(solution)/shard_map/all_to_all | solution.py:42
  111.4 6.6 %all-to-all-start.2 = ((bf16[2,1,256,128]{2,0,1,3:T(2,128)(2,1)}), bf16[2,1,256,128]{2,0,1,3:T(2,128)(2,1)S(1)}, u32[]{:S(2)}, u32[]{:S(2)}) async-start(bf16[2,1,256,128]{2,0,1,3:T(2,128)(2,1)} %copy.43), calls=%async_computation.2 | async-start | bytes 262144 | tf_op jit(solution)/shard_map/all_to_all | solution.py:74
  118.1 10.0 %all_gather.6 = bf16[2,1,1024,128]{2,3,0,1:T(8,128)(2,1)S(1)} all-gather(bf16[2,1,256,128]{2,3,0,1:T(8,128)(2,1)S(1)} %copy.38), channel_id=1, replica_groups=mesh['y'=4,'x_lo'=2,'z'=16,'x_hi'=2,'core'=2] {'x_hi','core'}, dimensions={2}, use_global_device_ids=true | all-gather | bytes 655360 | tf_op jit(solution)/shard_map/all_gather | solution.py:46
  128.1 5.5 all-to-all-done.2
  133.6 11.5 %all_gather.7 = bf16[2,1,1024,128]{2,3,0,1:T(8,128)(2,1)S(1)} all-gather(bf16[2,1,256,128]{2,3,0,1:T(8,128)(2,1)S(1)} %copy.44), channel_id=1, replica_groups=mesh['y'=4,'x_lo'=2,'z'=16,'x_hi'=2,'core'=2] {'x_hi','core'}, dimensions={2}, use_global_device_ids=true | all-gather | bytes 655360 | tf_op jit(solution)/shard_map/all_gather | solution.py:78
  145.1 2.3 fusion.6
  147.4 1.0 copy-done.3
  148.4 1.6 fusion.14
  150.0 4.5 fusion.17
  154.5 52.4 %all-reduce.19.cloned.1.call-done = (bf16[1024,2,1,128]{0,3,1,2:T(8,128)(2,1)}, bf16[1024,2,1,128]{0,3,1,2:T(8,128)(2,1)}) async-done(((bf16[1024,2,1,128]{0,3,1,2:T(8,128)(2,1)}, bf16[1024,2,1,128]{0,3,1,2:T(8,128)(2,1)}), (bf16[1024,2,1,128]{0,3,1,2:T(8,128)(2,1)}, bf16[1024,2,1,128]{0,3,1,2:T(8,128)(2,1)})) %all-reduce.19.cloned.1.call-update) | async-done | bytes 1048592 | tf_op jit(solution)/shard_map/psum | solution.py:52
  207.0 0.9 convert_convert_fusion
  208.7 16.6 %all-to-all-start.3 = ((bf16[256,2,1,128]{0,1,2,3:T(2,128)(2,1)}), bf16[256,2,1,128]{0,1,2,3:T(2,128)(2,1)S(1)}, u32[]{:S(2)}, u32[]{:S(2)}) async-start(bf16[256,2,1,128]{0,1,2,3:T(2,128)(2,1)} %copy.45), calls=%async_computation.3 | async-start | bytes 262144 | tf_op jit(solution)/shard_map/all_to_all | solution.py:93
  225.3 0.9 convert_convert_fusion.1
  227.0 15.0 %all-to-all-done.3 = bf16[256,2,1,128]{0,1,2,3:T(2,128)(2,1)S(1)} async-done(((bf16[256,2,1,128]{0,1,2,3:T(2,128)(2,1)}), bf16[256,2,1,128]{0,1,2,3:T(2,128)(2,1)S(1)}, u32[]{:S(2)}, u32[]{:S(2)}) %all-to-all-start.3) | async-done | bytes 131104 | tf_op jit(solution)/shard_map/all_to_all | solution.py:93
  242.0 6.8 %all-to-all-start.1 = ((bf16[256,2,1,128]{0,1,2,3:T(2,128)(2,1)}), bf16[256,2,1,128]{0,1,2,3:T(2,128)(2,1)S(1)}, u32[]{:S(2)}, u32[]{:S(2)}) async-start(bf16[256,2,1,128]{0,1,2,3:T(2,128)(2,1)} %copy.39), calls=%async_computation.1 | async-start | bytes 262144 | tf_op jit(solution)/shard_map/all_to_all | solution.py:61
  250.3 14.1 %all-to-all-done.1 = bf16[256,2,1,128]{0,1,2,3:T(2,128)(2,1)S(1)} async-done(((bf16[256,2,1,128]{0,1,2,3:T(2,128)(2,1)}), bf16[256,2,1,128]{0,1,2,3:T(2,128)(2,1)S(1)}, u32[]{:S(2)}, u32[]{:S(2)}) %all-to-all-start.1) | async-done | bytes 131104 | tf_op jit(solution)/shard_map/all_to_all | solution.py:61
  265.8 48.2 %all-reduce.17.cloned.1.call-done = (bf16[1,196,256]{2,1,0:T(8,128)(2,1)}, bf16[1,196,256]{2,1,0:T(8,128)(2,1)}) async-done(((bf16[1,196,256]{2,1,0:T(8,128)(2,1)}, bf16[1,196,256]{2,1,0:T(8,128)(2,1)}), (bf16[1,196,256]{2,1,0:T(8,128)(2,1)}, bf16[1,196,256]{2,1,0:T(8,128)(2,1)})) %all-reduce.17.cloned.1.call-update) | async-done | bytes 200720 | tf_op jit(solution)/shard_map/psum | solution.py:99
  314.0 1.2 fusion.51
  315.2 1.1 fusion.65
  316.3 0.9 convolution_bitcast_fusion
  317.3 126.5 %all-reduce.11.cloned.1.call-done = f32[256,256]{0,1:T(8,128)} async-done(((f32[256,256]{0,1:T(8,128)}), f32[256,256]{0,1:T(8,128)}) %all-reduce.11.cloned.1.call-update) | async-done | bytes 262160 | tf_op jit(solution)/shard_map/psum | solution.py:112
  443.9 0.9 fusion.20
  444.8 62.7 %all-reduce.13.cloned.1.call-done = f32[256,256]{0,1:T(8,128)} async-done(((f32[256,256]{0,1:T(8,128)}), f32[256,256]{0,1:T(8,128)}) %all-reduce.13.cloned.1.call-update) | async-done | bytes 262160 | tf_op jit(solution)/shard_map/psum | solution.py:112
  507.7 0.9 fusion.21
  508.6 49.1 %all-reduce.15.cloned.1.call-done = f32[256,256]{0,1:T(8,128)} async-done(((f32[256,256]{0,1:T(8,128)}), f32[256,256]{0,1:T(8,128)}) %all-reduce.15.cloned.1.call-update) | async-done | bytes 262160 | tf_op jit(solution)/shard_map/psum | solution.py:112
  557.6 1.8 copy.52
  (66 shorter events, 7.6 us)
Async XLA Ops:
  7.2 141.2 %copy-start = (bf16[1,1024,1024]{2,1,0:T(8,128)(2,1)S(1)}, bf16[1,1024,1024]{2,1,0:T(8,128)(2,1)}, u32[]{:S(2)}) copy-start(bf16[1,1024,1024]{2,1,0:T(8,128)(2,1)} %param.8) | copy-start | bytes 6291460
  7.2 69.9 %copy-start.2 = (bf16[196,256]{1,0:T(8,128)(2,1)S(1)}, bf16[196,256]{1,0:T(8,128)(2,1)}, u32[]{:S(2)}) copy-start(bf16[196,256]{1,0:T(8,128)(2,1)} %param.5) | copy-start | bytes 301060
  7.2 87.9 %copy-start.5 = (bf16[196,256]{1,0:T(8,128)(2,1)S(1)}, bf16[196,256]{1,0:T(8,128)(2,1)}, u32[]{:S(2)}) copy-start(bf16[196,256]{1,0:T(8,128)(2,1)} %param.9) | copy-start | bytes 301060
  7.2 66.2 %all-reduce.9.cloned.1.call-start = ((), (), s32[]{:S(2)}) async-start(), calls=%async_computation.4 | async-start | bytes 409600 | tf_op jit(solution)/shard_map/psum | solution.py:34
  74.5 2.2 copy-start.7
  74.5 2.2 copy-start.9
  75.6 1.1 copy-start.11
  75.6 1.1 copy-start.13
  78.1 33.3 %all-to-all-start = ((bf16[2,1,256,128]{2,0,1,3:T(2,128)(2,1)}), bf16[2,1,256,128]{2,0,1,3:T(2,128)(2,1)S(1)}, u32[]{:S(2)}, u32[]{:S(2)}) async-start(bf16[2,1,256,128]{2,0,1,3:T(2,128)(2,1)} %copy.37), calls=%async_computation | async-start | bytes 262144 | tf_op jit(solution)/shard_map/all_to_all | solution.py:42
  111.4 22.2 %all-to-all-start.2 = ((bf16[2,1,256,128]{2,0,1,3:T(2,128)(2,1)}), bf16[2,1,256,128]{2,0,1,3:T(2,128)(2,1)S(1)}, u32[]{:S(2)}, u32[]{:S(2)}) async-start(bf16[2,1,256,128]{2,0,1,3:T(2,128)(2,1)} %copy.43), calls=%async_computation.2 | async-start | bytes 262144 | tf_op jit(solution)/shard_map/all_to_all | solution.py:74
  118.1 88.9 %all-reduce.19.cloned.1.call-start = ((), (), s32[]{:S(2)}) async-start(), calls=%async_computation.9 | async-start | bytes 2097152 | tf_op jit(solution)/shard_map/psum | solution.py:52
  147.4 1.0 copy-start.3
  154.5 110.0 %copy-start.6 = (bf16[196,256]{1,0:T(8,128)(2,1)S(1)}, bf16[196,256]{1,0:T(8,128)(2,1)}, u32[]{:S(2)}) copy-start(bf16[196,256]{1,0:T(8,128)(2,1)} %param.9) | copy-start | bytes 301060
  207.9 106.2 %copy-start.1 = (f32[1,196,256]{2,1,0:T(8,128)S(1)}, f32[1,196,256]{2,1,0:T(8,128)}, u32[]{:S(2)}) copy-start(f32[1,196,256]{2,1,0:T(8,128)} %all-reduce.9.cloned.1.call-done) | copy-start | bytes 602116
  207.9 106.1 %copy-start.8 = (f32[256]{0:T(256)S(1)}, f32[256]{0:T(256)}, u32[]{:S(2)}) copy-start(f32[256]{0:T(256)} %copy-done.7) | copy-start | bytes 3076
  207.9 106.1 %copy-start.10 = (f32[196]{0:T(256)S(1)}, f32[196]{0:T(256)}, u32[]{:S(2)}) copy-start(f32[196]{0:T(256)} %copy-done.9) | copy-start | bytes 2356
  207.9 106.1 %copy-start.12 = (f32[256]{0:T(256)S(1)}, f32[256]{0:T(256)}, u32[]{:S(2)}) copy-start(f32[256]{0:T(256)} %copy-done.11) | copy-start | bytes 3076
  207.9 106.1 %copy-start.14 = (f32[196]{0:T(256)S(1)}, f32[196]{0:T(256)}, u32[]{:S(2)}) copy-start(f32[196]{0:T(256)} %copy-done.13) | copy-start | bytes 2356
  208.7 33.3 %all-to-all-start.3 = ((bf16[256,2,1,128]{0,1,2,3:T(2,128)(2,1)}), bf16[256,2,1,128]{0,1,2,3:T(2,128)(2,1)S(1)}, u32[]{:S(2)}, u32[]{:S(2)}) async-start(bf16[256,2,1,128]{0,1,2,3:T(2,128)(2,1)} %copy.45), calls=%async_computation.3 | async-start | bytes 262144 | tf_op jit(solution)/shard_map/all_to_all | solution.py:93
  242.0 22.3 %all-to-all-start.1 = ((bf16[256,2,1,128]{0,1,2,3:T(2,128)(2,1)}), bf16[256,2,1,128]{0,1,2,3:T(2,128)(2,1)S(1)}, u32[]{:S(2)}, u32[]{:S(2)}) async-start(bf16[256,2,1,128]{0,1,2,3:T(2,128)(2,1)} %copy.39), calls=%async_computation.1 | async-start | bytes 262144 | tf_op jit(solution)/shard_map/all_to_all | solution.py:61
  248.8 65.2 %all-reduce.17.cloned.1.call-start = ((), (), s32[]{:S(2)}) async-start(), calls=%async_computation.8 | async-start | bytes 409600 | tf_op jit(solution)/shard_map/psum | solution.py:99
  264.5 243.2 %copy-start.4 = (bf16[256,256]{1,0:T(8,128)(2,1)S(1)}, bf16[256,256]{1,0:T(8,128)(2,1)}, u32[]{:S(2)}) copy-start(bf16[256,256]{1,0:T(8,128)(2,1)} %param.6) | copy-start | bytes 393220
  265.8 178.0 %all-reduce.11.cloned.1.call-start = ((), (), s32[]{:S(2)}) async-start(), calls=%async_computation.5 | async-start | bytes 524288 | tf_op jit(solution)/shard_map/psum | solution.py:112
  317.3 190.1 %all-reduce.13.cloned.1.call-start = ((), (), s32[]{:S(2)}) async-start(), calls=%async_computation.6 | async-start | bytes 524288 | tf_op jit(solution)/shard_map/psum | solution.py:112
  443.9 113.8 %all-reduce.15.cloned.1.call-start = ((), (), s32[]{:S(2)}) async-start(), calls=%async_computation.7 | async-start | bytes 524288 | tf_op jit(solution)/shard_map/psum | solution.py:112
Sparse Core Ops, SparseCore 0:
  11.5 61.8 all-reduce.8
  154.7 52.2 all-reduce.18
  265.9 48.0 all-reduce.16
  317.4 126.3 all-reduce.10
  446.0 61.3 all-reduce.12
  510.2 47.4 all-reduce.14
where the time goes:
time: 567 us; the launch traced here: 566 us
  waiting for transfers between devices  453 us (80%)
  starting transfers between devices  46.9 us (8%)
  blocking collectives  21.4 us (4%)
  between operations  14.5 us (3%)
  matrix products  14.1 us (2%)
  local copies, waits for them, and re-layouts  8.99 us (2%)
  other arithmetic  7.34 us (1%)
    psum x3, waiting for transfers between devices, local(): grad_params = lax.psum(lax.psum(lax.psum(params_part, 'z'), 'y'), 'x_lo')  238 us
    psum x1, waiting for transfers between devices, local(): logits = lax.psum(partial_logits, HALF)  64.2 us
    psum x1, waiting for transfers between devices, local(): lax.psum(jnp.einsum('kf,sirk->fsir', down_slice, hidden, preferred_elemen...  52.4 us
    psum x1, waiting for transfers between devices, local(): lax.psum(dispatch_part.astype(jnp.bfloat16), HALF).astype(jnp.float32)  48.2 us
    all_to_all x1, starting transfers between devices, local(): lax.all_to_all(grad_slot_in.astype(jnp.bfloat16), EXPERT, split_axis=3, c...  16.6 us
    all_to_all x1, starting transfers between devices, local(): lax.all_to_all(slot_in, EXPERT, split_axis=3, concat_axis=3, tiled=True)  16.6 us
    all_to_all x1, waiting for transfers between devices, local(): lax.all_to_all(slot_in, EXPERT, split_axis=3, concat_axis=3, tiled=True)  15.3 us
    all_to_all x1, waiting for transfers between devices, local(): lax.all_to_all(grad_slot_in.astype(jnp.bfloat16), EXPERT, split_axis=3, c...  15 us
  transfers between devices with their start and end apart: 10, of which 10 were waited for; matrix products, arithmetic and copies ran while one was open for 1% of the time, Pallas kernels for 0%

commit v1 on v0

--- a/solution.py
+++ b/solution.py
@@ -49,11 +49,16 @@
     )
     hidden = jax.nn.gelu(preact).astype(jnp.bfloat16)
     down_slice = down_matrix
-    summed = lax.psum(
+
+    def direct_classes(frame_in, lane_axis, along_axis="x_hi"):
+        step_out = lax.psum(lax.psum(frame_in, axis_name=lane_axis), along_axis)
+        return step_out
+
+    summed = direct_classes(
         jnp.einsum("kf,sirk->fsir", down_slice, hidden, preferred_element_type=jnp.float32).astype(
             jnp.bfloat16
         ),
-        HALF,
+        "core",
     ).astype(jnp.float32)
     slot_out = lax.dynamic_slice_in_dim(
         summed, lax.axis_index(HALF) * feat_quarter, feat_quarter, 0

time: 567 us -> 635 us (1.12)
  waiting for transfers between devices: 453 us -> 512 us
  starting transfers between devices: 46.9 us -> 56.9 us
    psum x1 -> x3, waiting for transfers between devices: 52.4 us -> 125 us  [the longest x2 64.2 us: direct_classes(): step_out = lax.psum(lax.psum(frame_in, axis_name=lane_axis), along_axis)]
    all_to_all x1, waiting for transfers between devices: 15 us -> 0.01 us  [local(): lax.all_to_all(grad_slot_in.astype(jnp.bfloat16), EXPERT, split_axis=3, c...]
    all_to_all x1, starting transfers between devices: 6.81 us -> 16.8 us  [local(): lax.all_to_all(slot_out.astype(jnp.bfloat16), EXPERT, split_axis=3, conca...]
  transfers between devices with their start and end apart: 10 -> 12, of which waited for: 10 -> 11; matrix products, arithmetic and copies ran while one was open for 1% -> 2% of each run, Pallas kernels for 0% -> 0%
where the time goes in v1:
time: 635 us
  waiting for transfers between devices  512 us (81%)
  starting transfers between devices  56.9 us (9%)
  blocking collectives  21.4 us (3%)
  between operations  14.4 us (2%)
  matrix products  14.2 us (2%)
  local copies, waits for them, and re-layouts  8.94 us (1%)
  other arithmetic  7.32 us (1%)
    psum x3, waiting for transfers between devices, local(): grad_params = lax.psum(lax.psum(lax.psum(params_part, 'z'), 'y'), 'x_lo')  239 us
    psum x2, waiting for transfers between devices, direct_classes(): step_out = lax.psum(lax.psum(frame_in, axis_name=lane_axis), along_axis)  64.2 us
    psum x1, waiting for transfers between devices, local(): logits = lax.psum(partial_logits, HALF)  64.2 us
    psum x1, waiting for transfers between devices, local(): lax.psum(jnp.einsum('fk,sirk->fsir', up_slice, grad_preact, preferred_ele...  61.2 us
    psum x1, waiting for transfers between devices, local(): lax.psum(dispatch_part.astype(jnp.bfloat16), HALF).astype(jnp.float32)  48 us
    all_to_all x1, starting transfers between devices, local(): lax.all_to_all(slot_out.astype(jnp.bfloat16), EXPERT, split_axis=3, conca...  16.8 us
    all_to_all x1, starting transfers between devices, local(): lax.all_to_all(slot_in, EXPERT, split_axis=3, concat_axis=3, tiled=True)  16.6 us
    all_to_all x1, starting transfers between devices, local(): lax.all_to_all(grad_slot_in.astype(jnp.bfloat16), EXPERT, split_axis=3, c...  16.6 us
  transfers between devices with their start and end apart: 12, of which 11 were waited for; matrix products, arithmetic and copies ran while one was open for 2% of the time, Pallas kernels for 0%

profile of v1, /device:TPU:1, one launch (start us, length us, event | category | flops | bytes accessed | tf_op | source)
XLA Modules:
  0.0 634.7 jit_solution(14809448727358292391)
XLA Ops:
  7.2 2.0 convolution_bitcast_fusion.3
  9.2 64.2 %all-reduce.10.cloned.1.call-done = f32[1,196,256]{2,1,0:T(8,128)} async-done(((f32[1,196,256]{2,1,0:T(8,128)}), f32[1,196,256]{2,1,0:T(8,128)}) %all-reduce.10.cloned.1.call-update) | async-done | bytes 200720 | tf_op jit(solution)/shard_map/psum | solution.py:34
  73.4 1.0 fusion.82
  74.5 1.1 fusion.60
  75.6 1.1 fusion.80
  78.0 16.6 %all-to-all-start = ((bf16[2,1,256,128]{2,0,1,3:T(2,128)(2,1)}), bf16[2,1,256,128]{2,0,1,3:T(2,128)(2,1)S(1)}, u32[]{:S(2)}, u32[]{:S(2)}) async-start(bf16[2,1,256,128]{2,0,1,3:T(2,128)(2,1)} %copy.37), calls=%async_computation | async-start | bytes 262144 | tf_op jit(solution)/shard_map/all_to_all | solution.py:42
  96.0 15.3 %all-to-all-done = bf16[2,1,256,128]{2,0,1,3:T(2,128)(2,1)S(1)} async-done(((bf16[2,1,256,128]{2,0,1,3:T(2,128)(2,1)}), bf16[2,1,256,128]{2,0,1,3:T(2,128)(2,1)S(1)}, u32[]{:S(2)}, u32[]{:S(2)}) %all-to-all-start) | async-done | bytes 131104 | tf_op jit(solution)/shard_map/all_to_all | solution.py:42
  111.3 6.6 %all-to-all-start.2 = ((bf16[2,1,256,128]{2,0,1,3:T(2,128)(2,1)}), bf16[2,1,256,128]{2,0,1,3:T(2,128)(2,1)S(1)}, u32[]{:S(2)}, u32[]{:S(2)}) async-start(bf16[2,1,256,128]{2,0,1,3:T(2,128)(2,1)} %copy.43), calls=%async_computation.2 | async-start | bytes 262144 | tf_op jit(solution)/shard_map/all_to_all | solution.py:79
  118.1 10.0 %all_gather.6 = bf16[2,1,1024,128]{2,3,0,1:T(8,128)(2,1)S(1)} all-gather(bf16[2,1,256,128]{2,3,0,1:T(8,128)(2,1)S(1)} %copy.38), channel_id=1, replica_groups=mesh['y'=4,'x_lo'=2,'z'=16,'x_hi'=2,'core'=2] {'x_hi','core'}, dimensions={2}, use_global_device_ids=true | all-gather | bytes 655360 | tf_op jit(solution)/shard_map/all_gather | solution.py:46
  128.1 5.5 all-to-all-done.2
  133.5 11.5 %all_gather.7 = bf16[2,1,1024,128]{2,3,0,1:T(8,128)(2,1)S(1)} all-gather(bf16[2,1,256,128]{2,3,0,1:T(8,128)(2,1)S(1)} %copy.44), channel_id=1, replica_groups=mesh['y'=4,'x_lo'=2,'z'=16,'x_hi'=2,'core'=2] {'x_hi','core'}, dimensions={2}, use_global_device_ids=true | all-gather | bytes 655360 | tf_op jit(solution)/shard_map/all_gather | solution.py:83
  145.0 2.3 fusion.6
  147.3 1.0 copy-done.3
  148.3 1.6 fusion.14
  150.0 4.5 fusion.17
  154.6 27.7 %all-reduce.12.cloned.1.call-done = bf16[1024,2,1,128]{0,3,1,2:T(8,128)(2,1)} async-done(((bf16[1024,2,1,128]{0,3,1,2:T(8,128)(2,1)}), bf16[1024,2,1,128]{0,3,1,2:T(8,128)(2,1)}) %all-reduce.12.cloned.1.call-update) | async-done | bytes 524304 | tf_op jit(solution)/shard_map/psum | solution.py:54
  182.3 61.2 %all-reduce.16.cloned.1.call-done = bf16[1024,2,1,128]{0,3,1,2:T(8,128)(2,1)} async-done(((bf16[1024,2,1,128]{0,3,1,2:T(8,128)(2,1)}), bf16[1024,2,1,128]{0,3,1,2:T(8,128)(2,1)}) %all-reduce.16.cloned.1.call-update) | async-done | bytes 524304 | tf_op jit(solution)/shard_map/psum | solution.py:89
  243.6 0.9 convert_convert_fusion
  245.3 16.6 %all-to-all-start.3 = ((bf16[256,2,1,128]{0,1,2,3:T(2,128)(2,1)}), bf16[256,2,1,128]{0,1,2,3:T(2,128)(2,1)S(1)}, u32[]{:S(2)}, u32[]{:S(2)}) async-start(bf16[256,2,1,128]{0,1,2,3:T(2,128)(2,1)} %copy.45), calls=%async_computation.3 | async-start | bytes 262144 | tf_op jit(solution)/shard_map/all_to_all | solution.py:98
  261.9 36.5 %all-reduce.14.cloned.1.call-done = bf16[1024,2,1,128]{0,3,1,2:T(8,128)(2,1)} async-done(((bf16[1024,2,1,128]{0,3,1,2:T(8,128)(2,1)}), bf16[1024,2,1,128]{0,3,1,2:T(8,128)(2,1)}) %all-reduce.14.cloned.1.call-update) | async-done | bytes 524304 | tf_op jit(solution)/shard_map/psum | solution.py:54
  298.4 0.9 convert_convert_fusion.1
  300.1 16.8 %all-to-all-start.1 = ((bf16[256,2,1,128]{0,1,2,3:T(2,128)(2,1)}), bf16[256,2,1,128]{0,1,2,3:T(2,128)(2,1)S(1)}, u32[]{:S(2)}, u32[]{:S(2)}) async-start(bf16[256,2,1,128]{0,1,2,3:T(2,128)(2,1)} %copy.39), calls=%async_computation.1 | async-start | bytes 262144 | tf_op jit(solution)/shard_map/all_to_all | solution.py:66
  318.3 14.4 %all-to-all-done.1 = bf16[256,2,1,128]{0,1,2,3:T(2,128)(2,1)S(1)} async-done(((bf16[256,2,1,128]{0,1,2,3:T(2,128)(2,1)}), bf16[256,2,1,128]{0,1,2,3:T(2,128)(2,1)S(1)}, u32[]{:S(2)}, u32[]{:S(2)}) %all-to-all-start.1) | async-done | bytes 131104 | tf_op jit(solution)/shard_map/all_to_all | solution.py:66
  334.2 48.0 %all-reduce.24.cloned.1.call-done = (bf16[1,196,256]{2,1,0:T(8,128)(2,1)}, bf16[1,196,256]{2,1,0:T(8,128)(2,1)}) async-done(((bf16[1,196,256]{2,1,0:T(8,128)(2,1)}, bf16[1,196,256]{2,1,0:T(8,128)(2,1)}), (bf16[1,196,256]{2,1,0:T(8,128)(2,1)}, bf16[1,196,256]{2,1,0:T(8,128)(2,1)})) %all-reduce.24.cloned.1.call-update) | async-done | bytes 200720 | tf_op jit(solution)/shard_map/psum | solution.py:104
  382.2 1.2 fusion.51
  383.4 1.1 fusion.65
  384.5 0.9 convolution_bitcast_fusion
  385.5 126.5 %all-reduce.18.cloned.1.call-done = f32[256,256]{0,1:T(8,128)} async-done(((f32[256,256]{0,1:T(8,128)}), f32[256,256]{0,1:T(8,128)}) %all-reduce.18.cloned.1.call-update) | async-done | bytes 262160 | tf_op jit(solution)/shard_map/psum | solution.py:117
  512.3 63.5 %all-reduce.20.cloned.1.call-done = f32[256,256]{0,1:T(8,128)} async-done(((f32[256,256]{0,1:T(8,128)}), f32[256,256]{0,1:T(8,128)}) %all-reduce.20.cloned.1.call-update) | async-done | bytes 262160 | tf_op jit(solution)/shard_map/psum | solution.py:117
  575.8 0.9 fusion.20
  577.5 48.6 %all-reduce.22.cloned.1.call-done = f32[256,256]{0,1:T(8,128)} async-done(((f32[256,256]{0,1:T(8,128)}), f32[256,256]{0,1:T(8,128)}) %all-reduce.22.cloned.1.call-update) | async-done | bytes 262160 | tf_op jit(solution)/shard_map/psum | solution.py:117
  626.1 1.8 copy.52
  (56 shorter events, 8.6 us)
Async XLA Ops:
  7.2 141.1 %copy-start = (bf16[1,1024,1024]{2,1,0:T(8,128)(2,1)S(1)}, bf16[1,1024,1024]{2,1,0:T(8,128)(2,1)}, u32[]{:S(2)}) copy-start(bf16[1,1024,1024]{2,1,0:T(8,128)(2,1)} %param.8) | copy-start | bytes 6291460
  7.2 69.8 %copy-start.2 = (bf16[196,256]{1,0:T(8,128)(2,1)S(1)}, bf16[196,256]{1,0:T(8,128)(2,1)}, u32[]{:S(2)}) copy-start(bf16[196,256]{1,0:T(8,128)(2,1)} %param.5) | copy-start | bytes 301060
  7.2 87.8 %copy-start.5 = (bf16[196,256]{1,0:T(8,128)(2,1)S(1)}, bf16[196,256]{1,0:T(8,128)(2,1)}, u32[]{:S(2)}) copy-start(bf16[196,256]{1,0:T(8,128)(2,1)} %param.9) | copy-start | bytes 301060
  7.2 66.2 %all-reduce.10.cloned.1.call-start = ((), (), s32[]{:S(2)}) async-start(), calls=%async_computation.4 | async-start | bytes 409600 | tf_op jit(solution)/shard_map/psum | solution.py:34
  78.0 33.3 %all-to-all-start = ((bf16[2,1,256,128]{2,0,1,3:T(2,128)(2,1)}), bf16[2,1,256,128]{2,0,1,3:T(2,128)(2,1)S(1)}, u32[]{:S(2)}, u32[]{:S(2)}) async-start(bf16[2,1,256,128]{2,0,1,3:T(2,128)(2,1)} %copy.37), calls=%async_computation | async-start | bytes 262144 | tf_op jit(solution)/shard_map/all_to_all | solution.py:42
  111.3 22.2 %all-to-all-start.2 = ((bf16[2,1,256,128]{2,0,1,3:T(2,128)(2,1)}), bf16[2,1,256,128]{2,0,1,3:T(2,128)(2,1)S(1)}, u32[]{:S(2)}, u32[]{:S(2)}) async-start(bf16[2,1,256,128]{2,0,1,3:T(2,128)(2,1)} %copy.43), calls=%async_computation.2 | async-start | bytes 262144 | tf_op jit(solution)/shard_map/all_to_all | solution.py:79
  118.0 64.3 %all-reduce.12.cloned.1.call-start = ((), (), s32[]{:S(2)}) async-start(), calls=%async_computation.5 | async-start | bytes 1048576 | tf_op jit(solution)/shard_map/psum | solution.py:54
  147.3 1.0 copy-start.3
  150.0 93.6 %all-reduce.16.cloned.1.call-start = ((), (), s32[]{:S(2)}) async-start(), calls=%async_computation.7 | async-start | bytes 1048576 | tf_op jit(solution)/shard_map/psum | solution.py:89
  154.5 178.3 %copy-start.6 = (bf16[196,256]{1,0:T(8,128)(2,1)S(1)}, bf16[196,256]{1,0:T(8,128)(2,1)}, u32[]{:S(2)}) copy-start(bf16[196,256]{1,0:T(8,128)(2,1)} %param.9) | copy-start | bytes 301060
  154.6 143.8 %all-reduce.14.cloned.1.call-start = ((), (), s32[]{:S(2)}) async-start(), calls=%async_computation.6 | async-start | bytes 1048576 | tf_op jit(solution)/shard_map/psum | solution.py:54
  244.5 137.7 %copy-start.1 = (f32[1,196,256]{2,1,0:T(8,128)S(1)}, f32[1,196,256]{2,1,0:T(8,128)}, u32[]{:S(2)}) copy-start(f32[1,196,256]{2,1,0:T(8,128)} %all-reduce.10.cloned.1.call-done) | copy-start | bytes 602116
  245.3 54.8 %all-to-all-start.3 = ((bf16[256,2,1,128]{0,1,2,3:T(2,128)(2,1)}), bf16[256,2,1,128]{0,1,2,3:T(2,128)(2,1)S(1)}, u32[]{:S(2)}, u32[]{:S(2)}) async-start(bf16[256,2,1,128]{0,1,2,3:T(2,128)(2,1)} %copy.45), calls=%async_computation.3 | async-start | bytes 262144 | tf_op jit(solution)/shard_map/all_to_all | solution.py:98
  300.1 32.6 %all-to-all-start.1 = ((bf16[256,2,1,128]{0,1,2,3:T(2,128)(2,1)}), bf16[256,2,1,128]{0,1,2,3:T(2,128)(2,1)S(1)}, u32[]{:S(2)}, u32[]{:S(2)}) async-start(bf16[256,2,1,128]{0,1,2,3:T(2,128)(2,1)} %copy.39), calls=%async_computation.1 | async-start | bytes 262144 | tf_op jit(solution)/shard_map/all_to_all | solution.py:66
  316.9 65.3 %all-reduce.24.cloned.1.call-start = ((), (), s32[]{:S(2)}) async-start(), calls=%async_computation.11 | async-start | bytes 409600 | tf_op jit(solution)/shard_map/psum | solution.py:104
  332.9 243.8 %copy-start.4 = (bf16[256,256]{1,0:T(8,128)(2,1)S(1)}, bf16[256,256]{1,0:T(8,128)(2,1)}, u32[]{:S(2)}) copy-start(bf16[256,256]{1,0:T(8,128)(2,1)} %param.6) | copy-start | bytes 393220
  334.2 177.8 %all-reduce.18.cloned.1.call-start = ((), (), s32[]{:S(2)}) async-start(), calls=%async_computation.8 | async-start | bytes 524288 | tf_op jit(solution)/shard_map/psum | solution.py:117
  385.5 190.3 %all-reduce.20.cloned.1.call-start = ((), (), s32[]{:S(2)}) async-start(), calls=%async_computation.9 | async-start | bytes 524288 | tf_op jit(solution)/shard_map/psum | solution.py:117
  512.0 114.1 %all-reduce.22.cloned.1.call-start = ((), (), s32[]{:S(2)}) async-start(), calls=%async_computation.10 | async-start | bytes 524288 | tf_op jit(solution)/shard_map/psum | solution.py:117
Sparse Core Ops, SparseCore 0:
  11.5 61.8 all-reduce.9
  150.1 32.1 all-reduce.11
  185.3 58.2 all-reduce.15
  246.3 52.0 all-reduce.13
  334.3 47.8 all-reduce.23
  385.6 126.3 all-reduce.17
  514.3 61.3 all-reduce.19
  578.6 47.4 all-reduce.21
